TPU v7x, 32 devices: a whole 2x2x4 slice. The times are simulated.
32 devices in a mesh: gs: 8 (over z, y), img: 4 (over x, core).
Axes of the slice: x: 2, y: 2, z: 4, core: 2. Of those that a mesh axis runs over, the one named last changes fastest.
Arguments:
- gaussians: float32 [59, 40960], P(None, ('gs', 'img')), may hold values from -6 to 2048, as said below
- send_slots: int32 [32, 2560], P(('gs', 'img')), may hold values from 0 to 1279, as said below
- tile_lists: int32 [32, 128, 512], P('img', 'gs'), may hold values from -1 to 2559, as said below
- truth: float32 [3, 512, 2048], P(None, 'img', 'gs'), may hold values from 0 to 1
Outputs:
- rendered: float32 [3, 512, 2048], P(None, 'img', 'gs')
- pixel_loss: float32 [512, 2048], P('img', 'gs')
Inputs may be any that keep to these rules, and one draw needn't show every extreme that they name: `gaussians`: rows 0 and 1 are pixel positions, row 2 a depth of 10 to 60, rows 3 to 5 log scales, rows 6 to 9 a quaternion whose first component is at least 0.5, row 10 an opacity logit, rows 11 to 58 colour harmonics, 16 for each channel. `send_slots`: row s lists, for each destination device in order, 80 indices of source s's own Gaussians. `tile_lists`: live entries (0 or more) name distinct slots of the owning device's received Gaussians and come first, ordered by increasing depth (row 2) of the Gaussians they name; the rest are -1.
All inputs are finite; a program needn't handle non-finite values.
Results may differ from a plain program's by a relative error of at most 0.0003.
Values sent between devices are 32-bit elements; how exact they have to be, the bound alone decides.
No kernel may reach another device: no remote copies, remote signals or barrier semaphores. Data moves between devices by JAX's collectives and lax.ppermute only.
A program may use at most 64 MiB of HBM per device.

v0:
```python
import functools

import jax
import jax.numpy as jnp
import numpy as np
from jax import lax
from jax.experimental import pallas as pl
from jax.experimental.pallas import tpu as pltpu
from jax.sharding import PartitionSpec as P

TILE = 16
LANES = 128
SUBS = 8
PARAMS = 9
UNROLL = 16
LOG2E = 1.4426950408889634

coef_zero = 0.28209479177387814
coef_one = 0.4886025119029199
coef_two = [
    1.0925484305920792,
    -1.0925484305920792,
    0.31539156525252005,
    -1.0925484305920792,
    0.5462742152960396,
]
coef_three = [
    -0.5900435899266435,
    2.890611442640554,
    -0.4570457994644658,
    0.3731763325901154,
    -0.4570457994644658,
    1.445305721320277,
    -0.5900435899266435,
]
camera_z = -3000.0
ssim_share = 0.2
stable_one = 0.0001
stable_two = 0.0009


def iota(shape, dim):
    return lax.broadcasted_iota(jnp.int32, shape, dim)


def lane_take(values, index):
    return jnp.take_along_axis(values, index, axis=1, mode="promise_in_bounds")


def sublane_take(values, index):
    return jnp.take_along_axis(values, index, axis=0, mode="promise_in_bounds")


def as_bf16(value):
    return value.astype(jnp.bfloat16).astype(jnp.float32)


def three_parts(value):
    high = as_bf16(value)
    rest = value - high
    middle = as_bf16(rest)
    return high, middle, rest - middle


def project(row):
    mean_x, mean_y, mean_z = row(0), row(1), row(2)
    squared = [jnp.exp(2.0 * row(3 + k)) for k in range(3)]
    quat = [row(6 + k) for k in range(4)]
    norm = jnp.sqrt(quat[0] * quat[0] + quat[1] * quat[1] + quat[2] * quat[2] + quat[3] * quat[3])
    quat_w, quat_x, quat_y, quat_z = [part / norm for part in quat]
    first = [
        1.0 - 2.0 * (quat_y * quat_y + quat_z * quat_z),
        2.0 * (quat_x * quat_y - quat_w * quat_z),
        2.0 * (quat_x * quat_z + quat_w * quat_y),
    ]
    second = [
        2.0 * (quat_x * quat_y + quat_w * quat_z),
        1.0 - 2.0 * (quat_x * quat_x + quat_z * quat_z),
        2.0 * (quat_y * quat_z - quat_w * quat_x),
    ]

    def weighted(left, right):
        return (
            left[0] * right[0] * squared[0]
            + left[1] * right[1] * squared[1]
            + left[2] * right[2] * squared[2]
        )

    cov_xx = weighted(first, first) + 0.3
    cov_xy = weighted(first, second)
    cov_yy = weighted(second, second) + 0.3
    determinant = cov_xx * cov_yy - cov_xy * cov_xy
    log_opacity = -LOG2E * jnp.log(1.0 + jnp.exp(-row(10)))
    delta_z = mean_z - camera_z
    length = jnp.sqrt(mean_x * mean_x + mean_y * mean_y + delta_z * delta_z)
    dir_x, dir_y, dir_z = (mean_x / length, mean_y / length, delta_z / length)
    sq_x, sq_y, sq_z = (dir_x * dir_x, dir_y * dir_y, dir_z * dir_z)
    prod_xy, prod_yz, prod_xz = (dir_x * dir_y, dir_y * dir_z, dir_x * dir_z)
    basis = [
        coef_zero * jnp.ones_like(dir_x),
        -coef_one * dir_y,
        coef_one * dir_z,
        -coef_one * dir_x,
        coef_two[0] * prod_xy,
        coef_two[1] * prod_yz,
        coef_two[2] * (2.0 * sq_z - sq_x - sq_y),
        coef_two[3] * prod_xz,
        coef_two[4] * (sq_x - sq_y),
        coef_three[0] * dir_y * (3.0 * sq_x - sq_y),
        coef_three[1] * prod_xy * dir_z,
        coef_three[2] * dir_y * (4.0 * sq_z - sq_x - sq_y),
        coef_three[3] * dir_z * (2.0 * sq_z - 3.0 * sq_x - 3.0 * sq_y),
        coef_three[4] * dir_x * (4.0 * sq_z - sq_x - sq_y),
        coef_three[5] * dir_z * (sq_x - sq_y),
        coef_three[6] * dir_x * (sq_x - 3.0 * sq_y),
    ]
    colours = []
    for channel in range(3):
        total = row(11 + 16 * channel) * basis[0]
        for k in range(1, 16):
            total = total + row(11 + 16 * channel + k) * basis[k]
        colours.append(jnp.maximum(total + 0.5, 0.0))
    return [
        mean_x,
        mean_y,
        (-0.5 * LOG2E) * (cov_yy / determinant),
        LOG2E * (cov_xy / determinant),
        (-0.5 * LOG2E) * (cov_xx / determinant),
        log_opacity,
    ] + colours


def pack_kernel(cap, gauss_ref, send_ref, out_ref, table_ref, index_ref):
    targets = out_ref.shape[0]
    chunks = gauss_ref.shape[1] // LANES
    spare = LANES - cap
    rows = project(lambda k: gauss_ref[k : k + 1, :])
    for k in range(PARAMS):
        table_ref[k : k + 1, :] = rows[k]
    lane = iota((SUBS, LANES), 1)
    sub = iota((SUBS, LANES), 0)
    send_chunks = send_ref.shape[1] // LANES
    for target in range(targets):
        chunk, shift = divmod(target * cap, LANES)

        def piece(c):
            c = min(c, send_chunks - 1)
            return jnp.broadcast_to(send_ref[0:1, c * LANES : (c + 1) * LANES], (SUBS, LANES))

        index = piece(chunk)
        if shift:
            index = jnp.where(
                lane < LANES - shift,
                pltpu.roll(index, LANES - shift, axis=1),
                pltpu.roll(piece(chunk + 1), LANES - shift, axis=1),
            )
        result = index
        for r in range(-(-cap // spare)):
            moved = pltpu.roll(index, (cap - r * spare) % LANES, axis=1)
            result = jnp.where((lane >= cap) & (sub == r), moved, result)
        index_ref[target] = result

    def one(target, carry):
        index = index_ref[target]
        low, high = index & (LANES - 1), index >> 7
        left = jnp.zeros((SUBS, LANES), jnp.float32)
        right = left
        for c in range(chunks):
            hit = high == c
            part = lane_take(table_ref[0:SUBS, c * LANES : (c + 1) * LANES], low)
            left = jnp.where(hit, part, left)
            last = jnp.broadcast_to(
                table_ref[SUBS : SUBS + 1, c * LANES : (c + 1) * LANES], (SUBS, LANES)
            )
            right = jnp.where(hit, lane_take(last, low), right)
        out_ref[target] = jnp.where(lane < cap, left, right)
        return carry

    lax.fori_loop(0, targets, one, 0)


def sort_kernel(
    cols_here,
    lists_ref,
    basis_in,
    truth_in,
    index_ref,
    meta_ref,
    centre_ref,
    basis_ref,
    truth_ref,
    sems,
):
    copies = [
        pltpu.make_async_copy(basis_in, basis_ref, sems.at[0]),
        pltpu.make_async_copy(truth_in, truth_ref, sems.at[1]),
    ]
    for copy in copies:
        copy.start()
    tiles, length = lists_ref.shape
    lists = lists_ref[...]
    live = jnp.sum((lists >= 0).astype(jnp.float32), axis=1, keepdims=True)
    live = jnp.broadcast_to(live, (tiles, tiles))
    down, across = iota((tiles, tiles), 0), iota((tiles, tiles), 1)
    live_row = jnp.sum(jnp.where(down == across, live, 0.0), axis=0, keepdims=True)
    ahead = (live > live_row) | ((live == live_row) & (down < across))
    rank_row = jnp.sum(ahead.astype(jnp.float32), axis=0, keepdims=True)
    behind = (live_row > live) | ((live_row == live) & (across < down))
    rank = jnp.sum(behind.astype(jnp.float32), axis=1, keepdims=True)
    select = (rank_row == down.astype(jnp.float32)).astype(jnp.float32)
    placed = (rank == across.astype(jnp.float32)).astype(jnp.float32)
    live_sorted = jnp.sum(placed * live, axis=0, keepdims=True)
    tile_sorted = jnp.sum(placed * down.astype(jnp.float32), axis=0, keepdims=True)
    tile_id = tile_sorted.astype(jnp.int32)
    row_of = lax.div(tile_id, cols_here)
    column = (tile_id - row_of * cols_here) * TILE
    busy = jnp.sum((live > (LANES * across).astype(jnp.float32)).astype(jnp.int32), axis=0, keepdims=True)
    meta_ref[0:1, :] = live_sorted.astype(jnp.int32)
    meta_ref[1:2, :] = row_of * (TILE // SUBS * (cols_here * TILE // LANES)) + (column >> 7)
    meta_ref[2:3, :] = column & (LANES - 1)
    meta_ref[4:5, :] = (busy + (2 * SUBS - 1)) >> 4
    tile = jnp.sum(select * across.astype(jnp.float32), axis=1, keepdims=True).astype(jnp.int32)
    tile = jnp.broadcast_to(tile, (tiles, tiles))
    tile_row = lax.div(tile, cols_here)
    tile_col = tile - tile_row * cols_here
    tile_row = tile_row + lax.axis_index("img") * (tiles // cols_here)
    tile_col = tile_col + lax.axis_index("gs") * cols_here
    centre_ref[0] = (tile_col * TILE + TILE // 2).astype(jnp.float32)
    centre_ref[1] = (tile_row * TILE + TILE // 2).astype(jnp.float32)
    high = (lists >> 7).astype(jnp.float32).astype(jnp.bfloat16)
    low = (lists & (LANES - 1)).astype(jnp.float32).astype(jnp.bfloat16)
    select = select.astype(jnp.bfloat16)
    high = jnp.dot(select, high, preferred_element_type=jnp.float32)
    low = jnp.dot(select, low, preferred_element_type=jnp.float32)
    index_ref[...] = high.astype(jnp.int32) * LANES + low.astype(jnp.int32)
    for copy in copies:
        copy.wait()


def basis_matrix():
    local = np.arange(TILE) - 7.5
    kinds = [[(0, local**0), (1, local), (2, local**2)], [(3, local**0), (4, local)]]
    kinds += [[(k, local**0)] for k in range(5, 9)]
    matrix = np.zeros((2 * LANES, len(kinds) * LANES), np.float32)
    for kind, terms in enumerate(kinds):
        for coefficient, values in terms:
            for part in range(3):
                for t in range(SUBS):
                    start = kind * LANES + t * TILE
                    matrix[(coefficient * 3 + part) * SUBS + t, start : start + TILE] = values
    return jnp.asarray(matrix, jnp.bfloat16)


def render_kernel(
    cap,
    meta_ref,
    recv_ref,
    index_ref,
    centre_ref,
    basis_ref,
    truth_ref,
    out_ref,
    near_ref,
    far_ref,
    table_ref,
    rows_ref,
    image_ref,
):
    wide = out_ref.shape[2] // LANES
    sources = recv_ref.shape[0]
    tiles, list_len = index_ref.shape
    chunks = table_ref.shape[1] // LANES
    spare = LANES - cap
    lane = iota((SUBS, LANES), 1)
    sub = iota((SUBS, LANES), 0)
    for source in range(sources):
        value = recv_ref[source]
        last = jnp.zeros((SUBS, LANES), jnp.float32)
        for r in range(-(-cap // spare)):
            row = jnp.broadcast_to(value[r : r + 1, :], (SUBS, LANES))
            moved = pltpu.roll(row, (r * spare - cap) % LANES, axis=1)
            last = jnp.where((lane >= r * spare) & (lane < (r + 1) * spare), moved, last)
        chunk, shift = divmod(source * cap, LANES)
        here = min(cap, LANES - shift)
        if shift:
            value = pltpu.roll(value, shift, axis=1)
            last = pltpu.roll(last, shift, axis=1)
        for c, start, end, lo in ((chunk, shift, shift + here, 0), (chunk + 1, 0, cap - here, 1)):
            if end > start:
                table_ref[0:SUBS, c * LANES + start : c * LANES + end] = value[:, start:end]
                table_ref[SUBS : SUBS + 1, c * LANES + start : c * LANES + end] = last[0:1, start:end]

    zero = jnp.zeros((SUBS, LANES), jnp.float32)

    def coefficients_of(g, b):
        start = pl.multiple_of(g * SUBS, SUBS)
        index = index_ref[pl.ds(start, SUBS), pl.ds(pl.multiple_of(b * LANES, LANES), LANES)]
        live = index >= 0
        safe = jnp.maximum(index, 0)
        low, high = safe & (LANES - 1), safe >> 7
        params = [zero] * PARAMS
        for c in range(chunks):
            hit = high == c
            for p in range(PARAMS):
                row = table_ref[p : p + 1, c * LANES : (c + 1) * LANES]
                part = lane_take(jnp.broadcast_to(row, (SUBS, LANES)), low)
                params[p] = jnp.where(hit, part, params[p])
        u = params[0] - centre_ref[0, pl.ds(start, SUBS), :]
        v = params[1] - centre_ref[1, pl.ds(start, SUBS), :]
        quad_x, quad_xy, quad_y = params[2:5]
        slope_x = quad_x * u
        slope_y = quad_y * v
        constant = params[5] + slope_x * u + slope_y * v + quad_xy * u * v
        values = [
            jnp.where(live, constant, -1e5),
            jnp.where(live, -2.0 * slope_x - quad_xy * v, 0.0),
            jnp.where(live, quad_x, 0.0),
            jnp.where(live, -2.0 * slope_y - quad_xy * u, 0.0),
            jnp.where(live, quad_xy, 0.0),
            jnp.where(live, quad_y, 0.0),
        ] + params[6:9]
        parts = [part for value in values for part in three_parts(value)]
        parts += [zero] * (2 * LANES // SUBS - len(parts))
        return jnp.concatenate(parts, axis=0).T.astype(jnp.bfloat16)

    def block(b, carry):
        def pair(p, inner):
            both = [coefficients_of(2 * p + k, b) for k in range(2)]
            result = jnp.dot(
                jnp.concatenate(both, axis=0), basis_ref[...], preferred_element_type=jnp.float32
            )
            for k in range(2):
                to = pl.ds(pl.multiple_of((2 * p + k) * list_len + b * LANES, LANES), LANES)
                for kind in range(6):
                    rows_ref[kind, to, :] = result[
                        k * LANES : (k + 1) * LANES, kind * LANES : (kind + 1) * LANES
                    ]
            return inner

        return lax.fori_loop(0, meta_ref[4, b], pair, carry)

    lax.fori_loop(0, list_len // LANES, block, 0)

    up = sub.astype(jnp.float32) + 0.5
    up_squared = up * up
    flip = (SUBS - 1) - sub
    one = jnp.ones((SUBS, LANES), jnp.float32)

    def group(g, carry):
        steps = (meta_ref[0, g * SUBS] + UNROLL - 1) // UNROLL
        first = g * list_len

        def many(s, state):
            left_a, left_b, ra, ga, ba, rb, gb, bb = state
            for q in range(UNROLL):
                def row(kind):
                    return rows_ref[kind, pl.ds(first + s * UNROLL + q, SUBS, stride=0), :]

                even = row(0) + up_squared * row(2)
                odd = up * row(1)
                alpha_a = jnp.exp2(even - odd)
                alpha_b = jnp.exp2(even + odd)
                weight_a = left_a * alpha_a
                weight_b = left_b * alpha_b
                left_a = left_a - weight_a
                left_b = left_b - weight_b
                red, green, blue = row(3), row(4), row(5)
                ra, ga, ba = ra + weight_a * red, ga + weight_a * green, ba + weight_a * blue
                rb, gb, bb = rb + weight_b * red, gb + weight_b * green, bb + weight_b * blue
            return left_a, left_b, ra, ga, ba, rb, gb, bb

        state = lax.fori_loop(0, steps, many, (one, one) + (zero,) * 6)
        halves = [sublane_take(value, flip) for value in state[2:5]] + list(state[5:8])
        for t in range(SUBS):
            place, shift = meta_ref[1, g * SUBS + t], meta_ref[2, g * SUBS + t]
            mask = (lane >= shift) & (lane < shift + TILE)
            for half in range(2):
                for channel in range(3):
                    moved = pltpu.roll(
                        halves[half * 3 + channel], (shift - t * TILE) & (LANES - 1), axis=1
                    )
                    pltpu.store(image_ref.at[channel, place + half * wide], moved, mask=mask)
        return carry

    lax.fori_loop(0, tiles // SUBS, group, 0)

    height = out_ref.shape[1]
    for channel in range(3):
        for r in range(height // SUBS):
            for c in range(wide):
                rows, columns = slice(r * SUBS, (r + 1) * SUBS), slice(c * LANES, (c + 1) * LANES)
                out_ref[channel, rows, columns] = image_ref[channel, r * wide + c]
    sides = [
        jnp.concatenate([out_ref[:, rows, :], truth_ref[:, rows, :]])
        for rows in (slice(0, SUBS), slice(height - SUBS, height))
    ]
    near_ref[...], far_ref[...] = by_parity("img", sides[1], sides[0])


def by_parity(axis, first, second):
    even = lax.axis_index(axis) & 1 == 0
    return jnp.where(even, first, second), jnp.where(even, second, first)


def arrived_sides(axis, near, far):
    index, size = lax.axis_index(axis), lax.axis_size(axis)
    before, after = by_parity(axis, far, near)
    return (
        jnp.where(index == 0, 0.0, before),
        jnp.where(index == size - 1, 0.0, after),
    )


def window():
    offsets = np.arange(11) - 5.0
    weights = np.exp(-offsets * offsets / 4.5)
    return [float(weight) for weight in weights / weights.sum()]


def filtered(load):
    weights = window()
    total = load(5) * weights[5]
    for k in range(5):
        total = total + (load(k) + load(10 - k)) * weights[k]
    return total


def products(image, truth):
    return [image, truth, image * image, truth * truth, image * truth]


def down_kernel(image_ref, truth_ref, out_ref, copy_ref, values_ref, sem):
    copy = pltpu.make_async_copy(image_ref, copy_ref, sem)
    copy.start()
    _, height, width = image_ref.shape
    wide = width // LANES
    for channel in range(3):
        for c in range(wide):
            columns = slice(c * LANES, (c + 1) * LANES)
            parts = products(image_ref[channel, :, columns], truth_ref[channel, :, columns])
            for kind, part in enumerate(parts):
                values_ref[(kind * 3 + channel) * wide + c] = part

    def one(slot, carry):
        for r in range(1, height // SUBS - 1):
            out_ref[slot, r * SUBS : (r + 1) * SUBS, :] = filtered(
                lambda k: values_ref[slot, r * SUBS - 5 + k : r * SUBS + 3 + k, :]
            )
        return carry

    lax.fori_loop(0, out_ref.shape[0], one, 0)
    copy.wait()


def turn_kernel(
    image_ref, truth_ref, near_in, far_in, down_ref, out_ref, near_ref, far_ref, values_ref
):
    _, height, width = image_ref.shape
    wide = width // LANES
    above, below = arrived_sides("img", near_in[...], far_in[...])
    for channel in range(3):
        for c in range(wide):
            columns = slice(c * LANES, (c + 1) * LANES)

            def cut(ref, which, rows):
                return ref[which, rows, columns]

            near, far = slice(0, 2 * SUBS), slice(height - 2 * SUBS, height)
            top = products(
                *(
                    jnp.concatenate([above[k, :, columns], cut(ref, channel, near)])
                    for ref, k in ((image_ref, channel), (truth_ref, channel + 3))
                )
            )
            bottom = products(
                *(
                    jnp.concatenate([cut(ref, channel, far), below[k, :, columns]])
                    for ref, k in ((image_ref, channel), (truth_ref, channel + 3))
                )
            )
            for kind in range(5):
                quantity = kind * 3 + channel
                values_ref[0] = top[kind]
                values_ref[1] = bottom[kind]
                ends = [
                    filtered(lambda k: values_ref[side, 3 + k : 3 + k + SUBS, :]) for side in range(2)
                ]
                middle = down_ref[quantity * wide + c, SUBS : height - SUBS, :]
                turned = jnp.concatenate([ends[0], middle, ends[1]], axis=0).T
                out_ref[quantity, columns, :] = turned


    near_ref[...], far_ref[...] = by_parity(
        "gs", out_ref[:, width - SUBS : width, :], out_ref[:, 0:SUBS, :]
    )


def similarity(parts):
    mean_r, mean_t, square_r, square_t, product = parts
    both, squares = mean_r * mean_t, mean_r * mean_r + mean_t * mean_t
    return (
        (2.0 * both + stable_one)
        * (2.0 * (product - both) + stable_two)
        / ((squares + stable_one) * (square_r + square_t - squares + stable_two))
    )


def across_kernel(turned_ref, out_ref):
    tiles = turned_ref.shape[1] // SUBS
    out_ref[...] = jnp.zeros_like(out_ref)

    def one(channel, carry):
        for r in range(1, tiles - 1):
            parts = [
                filtered(
                    lambda k: turned_ref[
                        kind * 3 + channel, r * SUBS - 5 + k : r * SUBS + 3 + k, :
                    ]
                )
                for kind in range(5)
            ]
            rows = slice(r * SUBS, (r + 1) * SUBS)
            out_ref[rows, :] = out_ref[rows, :] + similarity(parts)
        return carry

    lax.fori_loop(0, 3, one, 0)


def loss_kernel(
    turned_ref, near_in, far_in, sum_ref, image_ref, truth_ref, out_ref, values_ref
):
    length = turned_ref.shape[1]
    before, after = arrived_sides("gs", near_in[...], far_in[...])
    ends = []
    for side in range(2):
        total = None
        for channel in range(3):
            parts = []
            for kind in range(5):
                quantity = kind * 3 + channel
                if side == 0:
                    values_ref[0:SUBS] = before[quantity]
                    values_ref[SUBS : 3 * SUBS] = turned_ref[quantity, 0 : 2 * SUBS, :]
                else:
                    values_ref[0 : 2 * SUBS] = turned_ref[quantity, length - 2 * SUBS : length, :]
                    values_ref[2 * SUBS : 3 * SUBS] = after[quantity]
                parts.append(filtered(lambda k: values_ref[3 + k : 3 + k + SUBS, :]))
            value = similarity(parts)
            total = value if total is None else total + value
        ends.append(total)
    sums = jnp.concatenate([ends[0], sum_ref[SUBS : length - SUBS, :], ends[1]], axis=0)
    for c in range(length // LANES):
        columns = slice(c * LANES, (c + 1) * LANES)
        mean = sums[columns].T * (1.0 / 3.0)
        apart = [jnp.abs(image_ref[k, :, columns] - truth_ref[k, :, columns]) for k in range(3)]
        distance = (apart[0] + apart[1] + apart[2]) * (1.0 / 3.0)
        out_ref[:, columns] = (1.0 - ssim_share) * distance + ssim_share * (1.0 - mean)


def exchanged(near, far, axis, spare):
    axes = ("gs", "img")
    sizes = {name: lax.axis_size(name) for name in axes}
    size = sizes[axis]

    def flat(place):
        return place["gs"] * sizes["img"] + place["img"]

    pairs = [[], []]
    for along in range(size):
        for other in range(sizes[spare]):
            source = {axis: along, spare: other}
            pairs[0].append((flat(source), flat({axis: along ^ 1, spare: other})))
            if 0 < along < size - 1:
                target = {axis: ((along + 1) ^ 1) - 1, spare: other}
            else:
                target = {axis: along, spare: other ^ 1}
            pairs[1].append((flat(source), flat(target)))
    return lax.ppermute(near, axes, pairs[0]), lax.ppermute(far, axes, pairs[1])


def grant(mebibytes):
    return pltpu.CompilerParams(vmem_limit_bytes=mebibytes << 20)


VMEM = pl.BlockSpec(memory_space=pltpu.VMEM)
SMEM = pl.BlockSpec(memory_space=pltpu.SMEM)
ANY = pl.BlockSpec(memory_space=pl.ANY)


def on_device(gaussians, send_slots, tile_lists, truth):
    axes = ("gs", "img")
    devices = lax.axis_size(axes)
    cap = send_slots.shape[1] // devices
    count = gaussians.shape[1]
    rows_here, cols_here, list_len = tile_lists.shape
    tiles = rows_here * cols_here
    slots = send_slots.shape[1]
    packed = pl.pallas_call(
        functools.partial(pack_kernel, cap),
        out_shape=jax.ShapeDtypeStruct((devices, SUBS, LANES), jnp.float32),
        in_specs=[VMEM, VMEM],
        out_specs=VMEM,
        scratch_shapes=[
            pltpu.VMEM((2 * SUBS, count), jnp.float32),
            pltpu.VMEM((devices, SUBS, LANES), jnp.int32),
        ],
        compiler_params=grant(6),
        name="pack",
    )(gaussians, send_slots)
    arrived = lax.all_to_all(packed, axes, split_axis=0, concat_axis=0, tiled=True)
    basis = basis_matrix()
    index, meta, centre, basis, truth = pl.pallas_call(
        functools.partial(sort_kernel, cols_here),
        out_shape=(
            jax.ShapeDtypeStruct((tiles, list_len), jnp.int32),
            jax.ShapeDtypeStruct((SUBS, tiles), jnp.int32),
            jax.ShapeDtypeStruct((2, tiles, LANES), jnp.float32),
            jax.ShapeDtypeStruct(basis.shape, basis.dtype),
            jax.ShapeDtypeStruct(truth.shape, jnp.float32),
        ),
        in_specs=[VMEM, ANY, ANY],
        out_specs=(VMEM,) * 5,
        scratch_shapes=[pltpu.SemaphoreType.DMA((2,))],
        compiler_params=grant(6),
        name="order",
    )(tile_lists.reshape(tiles, list_len), basis, truth)
    height, width = rows_here * TILE, cols_here * TILE
    wide = width // LANES

    def arrays(*shapes):
        return tuple(jax.ShapeDtypeStruct(shape, jnp.float32) for shape in shapes)

    def call(kernel, name, inputs, outputs, scratch):
        return pl.pallas_call(
            kernel,
            out_shape=outputs if len(outputs) > 1 else outputs[0],
            in_specs=[VMEM] * inputs,
            out_specs=(VMEM,) * len(outputs) if len(outputs) > 1 else VMEM,
            scratch_shapes=[pltpu.VMEM(shape, jnp.float32) for shape in scratch],
            compiler_params=grant(9),
            name=name,
        )

    image, near, far = pl.pallas_call(
        functools.partial(render_kernel, cap),
        out_shape=arrays((3, height, width), (6, SUBS, width), (6, SUBS, width)),
        in_specs=[SMEM] + [VMEM] * 5,
        out_specs=(VMEM,) * 3,
        scratch_shapes=[
            pltpu.VMEM((2 * SUBS, -(-slots // LANES) * LANES), jnp.float32),
            pltpu.VMEM((6, tiles // SUBS * list_len + SUBS, LANES), jnp.float32),
            pltpu.VMEM((3, height // SUBS * wide, SUBS, LANES), jnp.float32),
        ],
        compiler_params=grant(34),
        name="render",
    )(meta, arrived, index, centre, basis, truth)
    near, far = exchanged(near, far, "img", "gs")
    sums, rendered = pl.pallas_call(
        down_kernel,
        out_shape=arrays((15 * wide, height, LANES), (3, height, width)),
        in_specs=[VMEM, VMEM],
        out_specs=(VMEM, ANY),
        scratch_shapes=[
            pltpu.VMEM((15 * wide, height, LANES), jnp.float32),
            pltpu.SemaphoreType.DMA,
        ],
        compiler_params=grant(9),
        name="down",
    )(image, truth)
    turned, near, far = call(
        turn_kernel,
        "turn",
        5,
        arrays((15, width, height), (15, SUBS, height), (15, SUBS, height)),
        [(2, 3 * SUBS, LANES)],
    )(image, truth, near, far, sums)
    near, far = exchanged(near, far, "gs", "img")
    similar = call(across_kernel, "across", 1, arrays((width, height)), [])(turned)
    loss = call(loss_kernel, "loss", 6, arrays((height, width)), [(3 * SUBS, height)])(
        turned, near, far, similar, image, truth
    )
    return rendered, loss


def solution(mesh):
    return jax.shard_map(
        on_device,
        mesh=mesh,
        in_specs=(
            P(None, ("gs", "img")),
            P(("gs", "img"), None),
            P("img", "gs", None),
            P(None, "img", "gs"),
        ),
        out_specs=(P(None, "img", "gs"), P("img", "gs")),
        check_vma=False,
    )
```

profile of v0, /device:TPU:0, one launch (start us, length us, event | category | flops | bytes accessed | tf_op | source)
XLA Modules:
  0.0 55.1 jit_solution(1331047864555377557)
XLA Ops:
  0.6 0.0 copy-start.2
  0.6 1.0 %copy-done.2 = f32[59,1280]{1,0:T(8,128)S(1)} copy-done((f32[59,1280]{1,0:T(8,128)S(1)}, f32[59,1280]{1,0:T(8,128)}, u32[]{:S(2)}) %copy-start.2) | copy-done | bytes 302104
  1.6 0.0 copy-start.4
  1.6 0.7 %copy-done.4 = s32[1,2560]{1,0:T(1,128)S(1)} copy-done((s32[1,2560]{1,0:T(1,128)S(1)}, s32[1,2560]{1,0:T(1,128)}, u32[]{:S(2)}) %copy-start.4) | copy-done | bytes 10264
  2.3 4.0 %pack.1 = f32[32,8,128]{2,1,0:T(8,128)} custom-call(f32[59,1280]{1,0:T(8,128)S(1)} %copy-done.2, s32[1,2560]{1,0:T(1,128)S(1)} %copy-done.4), custom_call_target="tpu_custom_call" | custom-call | tf_op jit(solution)/shard_map/pack/pallas_call | solution.py:598
  6.3 7.3 %all-to-all-start = ((f32[32,8,128]{2,1,0:T(8,128)}), f32[32,8,128]{2,1,0:T(8,128)S(1)}, u32[]{:S(2)}, u32[]{:S(2)}) async-start(f32[32,8,128]{2,1,0:T(8,128)} %pack.1), calls=%async_computation | async-start | bytes 262144 | tf_op jit(solution)/shard_map/all_to_all | solution.py:610
  13.7 0.0 copy-start
  13.7 1.0 %copy-done = f32[3,128,256]{2,1,0:T(8,128)S(1)} copy-done((f32[3,128,256]{2,1,0:T(8,128)S(1)}, f32[3,128,256]{2,1,0:T(8,128)}, u32[]{:S(2)}) %copy-start) | copy-done | bytes 393240
  14.7 0.0 copy-start.1
  14.7 1.0 %copy-done.1 = bf16[256,768]{1,0:T(8,128)(2,1)S(1)} copy-done((bf16[256,768]{1,0:T(8,128)(2,1)S(1)}, bf16[256,768]{1,0:T(8,128)(2,1)}, u32[]{:S(2)}) %copy-start.1) | copy-done | bytes 393240
  15.6 0.0 copy-start.3
  15.6 0.9 %copy-done.3 = s32[8,16,512]{2,1,0:T(8,128)S(1)} copy-done((s32[8,16,512]{2,1,0:T(8,128)S(1)}, s32[8,16,512]{2,1,0:T(8,128)}, u32[]{:S(2)}) %copy-start.3) | copy-done | bytes 262168
  16.6 0.7 %order.1 = (s32[128,512]{1,0:T(8,128)S(1)}, s32[8,128]{1,0:T(8,128)S(1)}, f32[2,128,128]{2,1,0:T(8,128)S(1)}, bf16[256,768]{1,0:T(8,128)(2,1)S(1)}, f32[3,128,256]{2,1,0:T(8,128)S(1)}) custom-call(s32[128,512]{1,0:T(8,128)S(1)} %bitcast.1, bf16[256,768]{1,0:T(8,128)(2,1)S(1)} %copy-done.1, f32[3,128,256]{2,1,0:T(8,128)S(1)} %copy-done), custom_call_target="tpu_custom_call" | custom-call | tf_op jit(solution)/shard_map/order/pallas_call | solution.py:612
  17.3 4.5 %all-to-all-done.recv_ref = f32[32,8,128]{2,1,0:T(8,128)S(1)} async-done(((f32[32,8,128]{2,1,0:T(8,128)}), f32[32,8,128]{2,1,0:T(8,128)S(1)}, u32[]{:S(2)}, u32[]{:S(2)}) %all-to-all-start) | async-done | bytes 131104 | tf_op jit(solution)/shard_map/all_to_all | solution.py:610
  21.9 18.9 %render.1 = (f32[3,128,256]{2,1,0:T(8,128)S(1)}, f32[6,8,256]{2,1,0:T(8,128)S(1)}, f32[6,8,256]{2,1,0:T(8,128)S(1)}) custom-call(s32[8,128]{1,0:T(8,128)S(1)} %get-tuple-element.15.meta_ref, f32[32,8,128]{2,1,0:T(8,128)S(1)} %all-to-all-done.recv_ref, s32[128,512]{1,0:T(8,128)S(1)} %get-tuple-element.16.index_ref, ...), custom_call_target="tpu_custom_call" | custom-call | tf_op jit(solution)/shard_map/render/pallas_call | solution.py:644
  40.8 4.2 %collective-permute-start = (f32[6,8,256]{2,1,0:T(8,128)S(1)}, f32[6,8,256]{2,1,0:T(8,128)S(1)}, u32[]{:S(2)}, u32[]{:S(2)}) collective-permute-start(f32[6,8,256]{2,1,0:T(8,128)S(1)} %get-tuple-element.22), channel_id=1, source_target_pairs={{0,1},{4,5},{8,9},{12,13},{16,17},{20,21},{24,25},{28,29},{1,0},{5... | collective-permute-start | bytes 147464 | tf_op jit(solution)/shard_map/ppermute | solution.py:578
  45.0 0.0 collective-permute-start.1
  45.0 1.3 %down.1 = (f32[30,128,128]{2,1,0:T(8,128)S(1)}, f32[3,128,256]{2,1,0:T(8,128)}) custom-call(f32[3,128,256]{2,1,0:T(8,128)S(1)} %get-tuple-element.20.image_ref, f32[3,128,256]{2,1,0:T(8,128)S(1)} %get-tuple-element.19.truth_ref), custom_call_target="tpu_custom_call" | custom-call | tf_op jit(solution)/shard_map/down/pallas_call | solution.py:658
  46.3 0.0 collective-permute-done.near_in
  46.3 2.8 %collective-permute-done.1.far_in = f32[6,8,256]{2,1,0:T(8,128)S(1)} collective-permute-done((f32[6,8,256]{2,1,0:T(8,128)S(1)}, f32[6,8,256]{2,1,0:T(8,128)S(1)}, u32[]{:S(2)}, u32[]{:S(2)}) %collective-permute-start.1) | collective-permute-done | bytes 49184 | tf_op jit(solution)/shard_map/ppermute | solution.py:578
  49.1 0.7 %turn.1 = (f32[15,256,128]{2,1,0:T(8,128)S(1)}, f32[15,8,128]{2,1,0:T(8,128)S(1)}, f32[15,8,128]{2,1,0:T(8,128)S(1)}) custom-call(f32[3,128,256]{2,1,0:T(8,128)S(1)} %get-tuple-element.20.image_ref, f32[3,128,256]{2,1,0:T(8,128)S(1)} %get-tuple-element.19.truth_ref, f32[6,8,256]{2,1,0:T(8,128)S(1)} %collective-permute-done.near_in, ...), custom_call_target="tpu_custom_call" | custom-call | tf_op jit(solution)/shard_map/turn/pallas_call | solution.py:670
  49.8 0.1 collective-permute-start.2
  49.9 0.1 collective-permute-start.3
  49.9 1.5 %across.1.sum_ref = f32[256,128]{1,0:T(8,128)S(1)} custom-call(f32[15,256,128]{2,1,0:T(8,128)S(1)} %get-tuple-element.25.turned_ref), custom_call_target="tpu_custom_call" | custom-call | tf_op jit(solution)/shard_map/across/pallas_call | solution.py:678
  51.4 2.7 %collective-permute-done.2.near_in = f32[15,8,128]{2,1,0:T(8,128)S(1)} collective-permute-done((f32[15,8,128]{2,1,0:T(8,128)S(1)}, f32[15,8,128]{2,1,0:T(8,128)S(1)}, u32[]{:S(2)}, u32[]{:S(2)}) %collective-permute-start.2) | collective-permute-done | bytes 61472 | tf_op jit(solution)/shard_map/ppermute | solution.py:578
  54.1 0.0 collective-permute-done.3.far_in
  54.1 1.1 %loss.1 = f32[128,256]{1,0:T(8,128)} custom-call(f32[15,256,128]{2,1,0:T(8,128)S(1)} %get-tuple-element.25.turned_ref, f32[15,8,128]{2,1,0:T(8,128)S(1)} %collective-permute-done.2.near_in, f32[15,8,128]{2,1,0:T(8,128)S(1)} %collective-permute-done.3.far_in, f32[256,128]{1,0:T(8,128)S(1)} %across.1.sum_ref, f32[3,128,256]{2,1,0:T(8,128)S(1)} %get-tuple-element.20.image_ref, ...), custom_call_target="tpu_custom_call" | custom-call | tf_op jit(solution)/shard_map/loss/pallas_call | solution.py:679
Async XLA Ops:
  0.6 1.0 %copy-start.2 = (f32[59,1280]{1,0:T(8,128)S(1)}, f32[59,1280]{1,0:T(8,128)}, u32[]{:S(2)}) copy-start(f32[59,1280]{1,0:T(8,128)} %gauss_ref.1) | copy-start | bytes 906244
  1.6 0.7 %copy-start.4 = (s32[1,2560]{1,0:T(1,128)S(1)}, s32[1,2560]{1,0:T(1,128)}, u32[]{:S(2)}) copy-start(s32[1,2560]{1,0:T(1,128)} %send_ref.1) | copy-start | bytes 30724
  6.3 15.5 %all-to-all-start = ((f32[32,8,128]{2,1,0:T(8,128)}), f32[32,8,128]{2,1,0:T(8,128)S(1)}, u32[]{:S(2)}, u32[]{:S(2)}) async-start(f32[32,8,128]{2,1,0:T(8,128)} %pack.1), calls=%async_computation | async-start | bytes 262144 | tf_op jit(solution)/shard_map/all_to_all | solution.py:610
  13.7 1.0 %copy-start = (f32[3,128,256]{2,1,0:T(8,128)S(1)}, f32[3,128,256]{2,1,0:T(8,128)}, u32[]{:S(2)}) copy-start(f32[3,128,256]{2,1,0:T(8,128)} %truth_in.1) | copy-start | bytes 1179652
  14.7 1.0 %copy-start.1 = (bf16[256,768]{1,0:T(8,128)(2,1)S(1)}, bf16[256,768]{1,0:T(8,128)(2,1)}, u32[]{:S(2)}) copy-start(bf16[256,768]{1,0:T(8,128)(2,1)} %constant.2.clone.basis_in) | copy-start | bytes 1179652
  15.6 0.9 %copy-start.3 = (s32[8,16,512]{2,1,0:T(8,128)S(1)}, s32[8,16,512]{2,1,0:T(8,128)}, u32[]{:S(2)}) copy-start(s32[8,16,512]{2,1,0:T(8,128)} %param.7) | copy-start | bytes 786436
  40.8 5.5 %collective-permute-start = (f32[6,8,256]{2,1,0:T(8,128)S(1)}, f32[6,8,256]{2,1,0:T(8,128)S(1)}, u32[]{:S(2)}, u32[]{:S(2)}) collective-permute-start(f32[6,8,256]{2,1,0:T(8,128)S(1)} %get-tuple-element.22), channel_id=1, source_target_pairs={{0,1},{4,5},{8,9},{12,13},{16,17},{20,21},{24,25},{28,29},{1,0},{5... | collective-permute-start | bytes 147464 | tf_op jit(solution)/shard_map/ppermute | solution.py:578
  45.0 4.1 %collective-permute-start.1 = (f32[6,8,256]{2,1,0:T(8,128)S(1)}, f32[6,8,256]{2,1,0:T(8,128)S(1)}, u32[]{:S(2)}, u32[]{:S(2)}) collective-permute-start(f32[6,8,256]{2,1,0:T(8,128)S(1)} %get-tuple-element.23), channel_id=1, source_target_pairs={{0,4},{4,0},{8,12},{12,8},{16,20},{20,16},{24,28},{28,24},{1,2},{5... | collective-permute-start | bytes 147464 | tf_op jit(solution)/shard_map/ppermute | solution.py:578
  49.8 4.3 %collective-permute-start.2 = (f32[15,8,128]{2,1,0:T(8,128)S(1)}, f32[15,8,128]{2,1,0:T(8,128)S(1)}, u32[]{:S(2)}, u32[]{:S(2)}) collective-permute-start(f32[15,8,128]{2,1,0:T(8,128)S(1)} %get-tuple-element.26), channel_id=1, source_target_pairs={{0,4},{1,5},{2,6},{3,7},{4,0},{5,1},{6,2},{7,3},{8,12},{9,13},{10,... | collective-permute-start | bytes 184328 | tf_op jit(solution)/shard_map/ppermute | solution.py:578
  49.9 4.2 %collective-permute-start.3 = (f32[15,8,128]{2,1,0:T(8,128)S(1)}, f32[15,8,128]{2,1,0:T(8,128)S(1)}, u32[]{:S(2)}, u32[]{:S(2)}) collective-permute-start(f32[15,8,128]{2,1,0:T(8,128)S(1)} %get-tuple-element.27), channel_id=1, source_target_pairs={{0,1},{1,0},{2,3},{3,2},{4,8},{5,9},{6,10},{7,11},{8,4},{9,5},{10,... | collective-permute-start | bytes 184328 | tf_op jit(solution)/shard_map/ppermute | solution.py:578
where the time goes:
time: 55.3 us; the launch traced here: 55.1 us
  Pallas kernels  28.2 us (51%)
  starting transfers between devices  11.7 us (21%)
  waiting for transfers between devices  9.98 us (18%)
  local copies, waits for them, and re-layouts  4.6 us (8%)
  between operations  0.72 us (1%)
    pallas_call x1, Pallas kernels, on_device(): pl.pallas_call(functools.partial(render_kernel, cap), out_shape=arrays((3...  18.9 us
    all_to_all x1, starting transfers between devices, on_device(): lax.all_to_all(packed, axes, split_axis=0, concat_axis=0, tiled=True)  7.33 us
    unnamed x10, local copies, waits for them, and re-layouts  4.6 us
    all_to_all x1, waiting for transfers between devices, on_device(): lax.all_to_all(packed, axes, split_axis=0, concat_axis=0, tiled=True)  4.51 us
    ppermute x2, starting transfers between devices, exchanged(): lax.ppermute(near, axes, pairs[0])  4.26 us
    pallas_call x1, Pallas kernels, on_device(): pl.pallas_call(functools.partial(pack_kernel, cap), out_shape=jax.ShapeDt...  4.01 us
    ppermute x2, waiting for transfers between devices, exchanged(): lax.ppermute(far, axes, pairs[1])  2.82 us
    ppermute x2, waiting for transfers between devices, exchanged(): lax.ppermute(near, axes, pairs[0])  2.66 us
  transfers between devices with their start and end apart: 5, of which 3 were waited for; matrix products, arithmetic and copies ran while one was open for 0% of the time, Pallas kernels for 6%

commit v1 on v0

--- a/solution.py
+++ b/solution.py
@@ -13,6 +13,7 @@
 SUBS = 8
 PARAMS = 9
 UNROLL = 16
+FUSED = 64
 LOG2E = 1.4426950408889634
 
 coef_zero = 0.28209479177387814
@@ -130,16 +131,23 @@
     ] + colours
 
 
-def pack_kernel(cap, gauss_ref, send_ref, out_ref, table_ref, index_ref):
+def pack_kernel(
+    cap, gauss_in, send_in, out_ref, gauss_ref, send_ref, table_ref, index_ref, last_ref, sems
+):
+    copies = [
+        pltpu.make_async_copy(send_in, send_ref, sems.at[0]),
+        pltpu.make_async_copy(gauss_in, gauss_ref, sems.at[1]),
+    ]
+    for copy in copies:
+        copy.start()
     targets = out_ref.shape[0]
     chunks = gauss_ref.shape[1] // LANES
     spare = LANES - cap
-    rows = project(lambda k: gauss_ref[k : k + 1, :])
-    for k in range(PARAMS):
-        table_ref[k : k + 1, :] = rows[k]
+    extra_rows = -(-cap // spare)
     lane = iota((SUBS, LANES), 1)
     sub = iota((SUBS, LANES), 0)
     send_chunks = send_ref.shape[1] // LANES
+    copies[0].wait()
     for target in range(targets):
         chunk, shift = divmod(target * cap, LANES)
 
@@ -154,29 +162,38 @@
                 pltpu.roll(index, LANES - shift, axis=1),
                 pltpu.roll(piece(chunk + 1), LANES - shift, axis=1),
             )
-        result = index
-        for r in range(-(-cap // spare)):
-            moved = pltpu.roll(index, (cap - r * spare) % LANES, axis=1)
-            result = jnp.where((lane >= cap) & (sub == r), moved, result)
-        index_ref[target] = result
-
-    def one(target, carry):
-        index = index_ref[target]
+        index_ref[target : target + 1, :] = index[0:1, :]
+    copies[1].wait()
+    rows = project(lambda k: gauss_ref[k : k + 1, :])
+    for k in range(PARAMS):
+        table_ref[k : k + 1, :] = rows[k]
+
+    def gather(index, value_of):
         low, high = index & (LANES - 1), index >> 7
-        left = jnp.zeros((SUBS, LANES), jnp.float32)
-        right = left
+        total = jnp.zeros((SUBS, LANES), jnp.float32)
         for c in range(chunks):
-            hit = high == c
-            part = lane_take(table_ref[0:SUBS, c * LANES : (c + 1) * LANES], low)
-            left = jnp.where(hit, part, left)
-            last = jnp.broadcast_to(
-                table_ref[SUBS : SUBS + 1, c * LANES : (c + 1) * LANES], (SUBS, LANES)
-            )
-            right = jnp.where(hit, lane_take(last, low), right)
-        out_ref[target] = jnp.where(lane < cap, left, right)
+            part = lane_take(value_of(slice(c * LANES, (c + 1) * LANES)), low)
+            total = jnp.where(high == c, part, total)
+        return total
+
+    def octet(o, carry):
+        first = pl.multiple_of(o * SUBS, SUBS)
+        last = gather(
+            index_ref[pl.ds(first, SUBS), :],
+            lambda at: jnp.broadcast_to(table_ref[SUBS : SUBS + 1, at], (SUBS, LANES)),
+        )
+        for r in range(extra_rows):
+            last_ref[r, 0:SUBS, :] = pltpu.roll(last, (cap - r * spare) % LANES, axis=1)
+        for k in range(SUBS):
+            index = index_ref[pl.ds(first + k, SUBS, stride=0), :]
+            result = gather(index, lambda at: table_ref[0:SUBS, at])
+            for r in range(extra_rows):
+                row = last_ref[r, pl.ds(k, SUBS, stride=0), :]
+                result = jnp.where((lane >= cap) & (sub == r), row, result)
+            out_ref[first + k] = result
         return carry
 
-    lax.fori_loop(0, targets, one, 0)
+    lax.fori_loop(0, targets // SUBS, octet, 0)
 
 
 def sort_kernel(
@@ -263,7 +280,10 @@
     near_ref,
     far_ref,
     table_ref,
-    rows_ref,
+    rows_a,
+    rows_b,
+    stacked_a,
+    stacked_b,
     image_ref,
 ):
     wide = out_ref.shape[2] // LANES
@@ -323,53 +343,43 @@
         parts += [zero] * (2 * LANES // SUBS - len(parts))
         return jnp.concatenate(parts, axis=0).T.astype(jnp.bfloat16)
 
-    def block(b, carry):
-        def pair(p, inner):
-            both = [coefficients_of(2 * p + k, b) for k in range(2)]
-            result = jnp.dot(
-                jnp.concatenate(both, axis=0), basis_ref[...], preferred_element_type=jnp.float32
-            )
-            for k in range(2):
-                to = pl.ds(pl.multiple_of((2 * p + k) * list_len + b * LANES, LANES), LANES)
-                for kind in range(6):
-                    rows_ref[kind, to, :] = result[
-                        k * LANES : (k + 1) * LANES, kind * LANES : (kind + 1) * LANES
-                    ]
-            return inner
-
-        return lax.fori_loop(0, meta_ref[4, b], pair, carry)
-
-    lax.fori_loop(0, list_len // LANES, block, 0)
-
     up = sub.astype(jnp.float32) + 0.5
     up_squared = up * up
     flip = (SUBS - 1) - sub
     one = jnp.ones((SUBS, LANES), jnp.float32)
-
-    def group(g, carry):
-        steps = (meta_ref[0, g * SUBS] + UNROLL - 1) // UNROLL
-        first = g * list_len
-
-        def many(s, state):
-            left_a, left_b, ra, ga, ba, rb, gb, bb = state
-            for q in range(UNROLL):
-                def row(kind):
-                    return rows_ref[kind, pl.ds(first + s * UNROLL + q, SUBS, stride=0), :]
-
-                even = row(0) + up_squared * row(2)
-                odd = up * row(1)
-                alpha_a = jnp.exp2(even - odd)
-                alpha_b = jnp.exp2(even + odd)
-                weight_a = left_a * alpha_a
-                weight_b = left_b * alpha_b
-                left_a = left_a - weight_a
-                left_b = left_b - weight_b
-                red, green, blue = row(3), row(4), row(5)
-                ra, ga, ba = ra + weight_a * red, ga + weight_a * green, ba + weight_a * blue
-                rb, gb, bb = rb + weight_b * red, gb + weight_b * green, bb + weight_b * blue
-            return left_a, left_b, ra, ga, ba, rb, gb, bb
-
-        state = lax.fori_loop(0, steps, many, (one, one) + (zero,) * 6)
+    fresh = (one, one) + (zero,) * 6
+    groups = tiles // SUBS
+
+    def blend(rows_ref, first, amount, state):
+        left_a, left_b, ra, ga, ba, rb, gb, bb = state
+        for q in range(amount):
+            def row(kind):
+                return rows_ref[kind, pl.ds(first + q, SUBS, stride=0), :]
+
+            even = row(0) + up_squared * row(2)
+            odd = up * row(1)
+            alpha_a = jnp.exp2(even - odd)
+            alpha_b = jnp.exp2(even + odd)
+            weight_a = left_a * alpha_a
+            weight_b = left_b * alpha_b
+            left_a = left_a - weight_a
+            left_b = left_b - weight_b
+            red, green, blue = row(3), row(4), row(5)
+            ra, ga, ba = ra + weight_a * red, ga + weight_a * green, ba + weight_a * blue
+            rb, gb, bb = rb + weight_b * red, gb + weight_b * green, bb + weight_b * blue
+        return left_a, left_b, ra, ga, ba, rb, gb, bb
+
+    def expand(stacked_ref, rows_ref):
+        result = jnp.dot(stacked_ref[...], basis_ref[...], preferred_element_type=jnp.float32)
+        for kind in range(6):
+            rows_ref[kind, 0:LANES, :] = result[:, kind * LANES : (kind + 1) * LANES]
+
+    def following(at):
+        g, b = at
+        more = (b + 1) * LANES < meta_ref[0, g * SUBS]
+        return jnp.where(more, g, jnp.minimum(g + 1, groups - 1)), jnp.where(more, b + 1, 0)
+
+    def finish(g, state):
         halves = [sublane_take(value, flip) for value in state[2:5]] + list(state[5:8])
         for t in range(SUBS):
             place, shift = meta_ref[1, g * SUBS + t], meta_ref[2, g * SUBS + t]
@@ -380,9 +390,43 @@
                         halves[half * 3 + channel], (shift - t * TILE) & (LANES - 1), axis=1
                     )
                     pltpu.store(image_ref.at[channel, place + half * wide], moved, mask=mask)
-        return carry
-
-    lax.fori_loop(0, tiles // SUBS, group, 0)
+
+    def turn(now, ahead, state, rows_now, rows_next, stacked_next, stacked_free):
+        g, b = now
+        later = following(ahead)
+        state = tuple(jnp.where(b == 0, start, value) for start, value in zip(fresh, state))
+        state = blend(rows_now, 0, FUSED, state)
+        expand(stacked_next, rows_next)
+        stacked_free[...] = coefficients_of(*later)
+        count = meta_ref[0, g * SUBS] - b * LANES
+        rest = (jnp.clip(count - FUSED, 0, LANES - FUSED) + UNROLL - 1) // UNROLL
+
+        def many(s, inner):
+            return blend(rows_now, FUSED + s * UNROLL, UNROLL, inner)
+
+        state = lax.fori_loop(0, rest, many, state)
+
+        @pl.when(count <= LANES)
+        def _():
+            finish(g, state)
+
+        return ahead, later, state
+
+    def two(_, carry):
+        now, ahead, state = carry
+        now, ahead, state = turn(now, ahead, state, rows_a, rows_b, stacked_b, stacked_a)
+        return turn(now, ahead, state, rows_b, rows_a, stacked_a, stacked_b)
+
+    def add_blocks(g, total):
+        return total + jnp.maximum((meta_ref[0, g * SUBS] + LANES - 1) // LANES, 1)
+
+    blocks = lax.fori_loop(0, groups, add_blocks, 0)
+    start = (jnp.int32(0), jnp.int32(0))
+    second = following(start)
+    stacked_a[...] = coefficients_of(*start)
+    expand(stacked_a, rows_a)
+    stacked_b[...] = coefficients_of(*second)
+    lax.fori_loop(0, (blocks + 1) // 2, two, (start, second, fresh))
 
     height = out_ref.shape[1]
     for channel in range(3):
@@ -584,7 +628,7 @@
 
 VMEM = pl.BlockSpec(memory_space=pltpu.VMEM)
 SMEM = pl.BlockSpec(memory_space=pltpu.SMEM)
-ANY = pl.BlockSpec(memory_space=pl.ANY)
+ANY = pl.BlockSpec(memory_space=pltpu.HBM)
 
 
 def on_device(gaussians, send_slots, tile_lists, truth):
@@ -598,13 +642,17 @@
     packed = pl.pallas_call(
         functools.partial(pack_kernel, cap),
         out_shape=jax.ShapeDtypeStruct((devices, SUBS, LANES), jnp.float32),
-        in_specs=[VMEM, VMEM],
+        in_specs=[ANY, ANY],
         out_specs=VMEM,
         scratch_shapes=[
+            pltpu.VMEM(gaussians.shape, jnp.float32),
+            pltpu.VMEM(send_slots.shape, jnp.int32),
             pltpu.VMEM((2 * SUBS, count), jnp.float32),
-            pltpu.VMEM((devices, SUBS, LANES), jnp.int32),
+            pltpu.VMEM((devices + SUBS, LANES), jnp.int32),
+            pltpu.VMEM((SUBS, 2 * SUBS, LANES), jnp.float32),
+            pltpu.SemaphoreType.DMA((2,)),
         ],
-        compiler_params=grant(6),
+        compiler_params=grant(60),
         name="pack",
     )(gaussians, send_slots)
     arrived = lax.all_to_all(packed, axes, split_axis=0, concat_axis=0, tiled=True)
@@ -648,10 +696,13 @@
         out_specs=(VMEM,) * 3,
         scratch_shapes=[
             pltpu.VMEM((2 * SUBS, -(-slots // LANES) * LANES), jnp.float32),
-            pltpu.VMEM((6, tiles // SUBS * list_len + SUBS, LANES), jnp.float32),
+            pltpu.VMEM((6, LANES + SUBS, LANES), jnp.float32),
+            pltpu.VMEM((6, LANES + SUBS, LANES), jnp.float32),
+            pltpu.VMEM((LANES, 2 * LANES), jnp.bfloat16),
+            pltpu.VMEM((LANES, 2 * LANES), jnp.bfloat16),
             pltpu.VMEM((3, height // SUBS * wide, SUBS, LANES), jnp.float32),
         ],
-        compiler_params=grant(34),
+        compiler_params=grant(12),
         name="render",
     )(meta, arrived, index, centre, basis, truth)
     near, far = exchanged(near, far, "img", "gs")

time: 55.3 us -> 49 us (0.89)
  Pallas kernels: 28.2 us -> 24.7 us
  local copies, waits for them, and re-layouts: 4.6 us -> 2.94 us
  waiting for transfers between devices: 9.98 us -> 8.92 us
    pallas_call x1, Pallas kernels: 18.9 us -> 16.9 us  [on_device(): pl.pallas_call(functools.partial(render_kernel, cap), out_shape=arrays((3...]
    unnamed x10 -> x6, local copies, waits for them, and re-layouts: 4.6 us -> 2.94 us
    pallas_call x1, Pallas kernels: 4.01 us -> 2.62 us  [on_device(): pl.pallas_call(functools.partial(pack_kernel, cap), out_shape=jax.ShapeDt...]
    ppermute x2, starting transfers between devices: 4.26 us -> 3.53 us  [exchanged(): lax.ppermute(near, axes, pairs[0])]
    ppermute x2, waiting for transfers between devices: 2.82 us -> 2.24 us  [exchanged(): lax.ppermute(far, axes, pairs[1])]
  transfers between devices with their start and end apart: 5 -> 5, of which waited for: 3 -> 3; matrix products, arithmetic and copies ran while one was open for 0% -> 0% of each run, Pallas kernels for 6% -> 7%
where the time goes in v1:
time: 49 us; the launch traced here: 48.7 us
  Pallas kernels  24.7 us (50%)
  starting transfers between devices  11.4 us (23%)
  waiting for transfers between devices  8.92 us (18%)
  local copies, waits for them, and re-layouts  2.94 us (6%)
  between operations  0.7 us (1%)
    pallas_call x1, Pallas kernels, on_device(): pl.pallas_call(functools.partial(render_kernel, cap), out_shape=arrays((3...  16.9 us
    all_to_all x1, starting transfers between devices, on_device(): lax.all_to_all(packed, axes, split_axis=0, concat_axis=0, tiled=True)  7.33 us
    all_to_all x1, waiting for transfers between devices, on_device(): lax.all_to_all(packed, axes, split_axis=0, concat_axis=0, tiled=True)  4.51 us
    ppermute x2, starting transfers between devices, exchanged(): lax.ppermute(near, axes, pairs[0])  3.53 us
    unnamed x6, local copies, waits for them, and re-layouts  2.94 us
    pallas_call x1, Pallas kernels, on_device(): pl.pallas_call(functools.partial(pack_kernel, cap), out_shape=jax.ShapeDt...  2.62 us
    ppermute x2, waiting for transfers between devices, exchanged(): lax.ppermute(far, axes, pairs[1])  2.24 us
    ppermute x2, waiting for transfers between devices, exchanged(): lax.ppermute(near, axes, pairs[0])  2.17 us
  transfers between devices with their start and end apart: 5, of which 3 were waited for; matrix products, arithmetic and copies ran while one was open for 0% of the time, Pallas kernels for 7%

profile of v1, /device:TPU:0, one launch (start us, length us, event | category | flops | bytes accessed | tf_op | source)
XLA Modules:
  0.0 48.7 jit_solution(2582402684802093156)
XLA Ops:
  0.6 2.6 %pack.1 = f32[32,8,128]{2,1,0:T(8,128)} custom-call(f32[59,1280]{1,0:T(8,128)} %gauss_in.1, s32[1,2560]{1,0:T(1,128)} %send_in.1), custom_call_target="tpu_custom_call" | custom-call | tf_op jit(solution)/shard_map/pack/pallas_call | solution.py:642
  3.3 7.3 %all-to-all-start = ((f32[32,8,128]{2,1,0:T(8,128)}), f32[32,8,128]{2,1,0:T(8,128)S(1)}, u32[]{:S(2)}, u32[]{:S(2)}) async-start(f32[32,8,128]{2,1,0:T(8,128)} %pack.1), calls=%async_computation | async-start | bytes 262144 | tf_op jit(solution)/shard_map/all_to_all | solution.py:658
  10.6 0.0 copy-start
  10.6 1.0 %copy-done = f32[3,128,256]{2,1,0:T(8,128)S(1)} copy-done((f32[3,128,256]{2,1,0:T(8,128)S(1)}, f32[3,128,256]{2,1,0:T(8,128)}, u32[]{:S(2)}) %copy-start) | copy-done | bytes 393240
  11.6 0.0 copy-start.1
  11.6 1.0 %copy-done.1 = bf16[256,768]{1,0:T(8,128)(2,1)S(1)} copy-done((bf16[256,768]{1,0:T(8,128)(2,1)S(1)}, bf16[256,768]{1,0:T(8,128)(2,1)}, u32[]{:S(2)}) %copy-start.1) | copy-done | bytes 393240
  12.6 0.0 copy-start.2
  12.6 0.9 %copy-done.2 = s32[8,16,512]{2,1,0:T(8,128)S(1)} copy-done((s32[8,16,512]{2,1,0:T(8,128)S(1)}, s32[8,16,512]{2,1,0:T(8,128)}, u32[]{:S(2)}) %copy-start.2) | copy-done | bytes 262168
  13.5 0.7 %order.1 = (s32[128,512]{1,0:T(8,128)S(1)}, s32[8,128]{1,0:T(8,128)S(1)}, f32[2,128,128]{2,1,0:T(8,128)S(1)}, bf16[256,768]{1,0:T(8,128)(2,1)S(1)}, f32[3,128,256]{2,1,0:T(8,128)S(1)}) custom-call(s32[128,512]{1,0:T(8,128)S(1)} %bitcast.1, bf16[256,768]{1,0:T(8,128)(2,1)S(1)} %copy-done.1, f32[3,128,256]{2,1,0:T(8,128)S(1)} %copy-done), custom_call_target="tpu_custom_call" | custom-call | tf_op jit(solution)/shard_map/order/pallas_call | solution.py:660
  14.3 4.5 %all-to-all-done.recv_ref = f32[32,8,128]{2,1,0:T(8,128)S(1)} async-done(((f32[32,8,128]{2,1,0:T(8,128)}), f32[32,8,128]{2,1,0:T(8,128)S(1)}, u32[]{:S(2)}, u32[]{:S(2)}) %all-to-all-start) | async-done | bytes 131104 | tf_op jit(solution)/shard_map/all_to_all | solution.py:658
  18.8 16.9 %render.1 = (f32[3,128,256]{2,1,0:T(8,128)S(1)}, f32[6,8,256]{2,1,0:T(8,128)S(1)}, f32[6,8,256]{2,1,0:T(8,128)S(1)}) custom-call(s32[8,128]{1,0:T(8,128)S(1)} %get-tuple-element.15.meta_ref, f32[32,8,128]{2,1,0:T(8,128)S(1)} %all-to-all-done.recv_ref, s32[128,512]{1,0:T(8,128)S(1)} %get-tuple-element.16.index_ref, ...), custom_call_target="tpu_custom_call" | custom-call | tf_op jit(solution)/shard_map/render/pallas_call | solution.py:692
  35.7 2.9 %collective-permute-start = (f32[6,8,256]{2,1,0:T(8,128)S(1)}, f32[6,8,256]{2,1,0:T(8,128)S(1)}, u32[]{:S(2)}, u32[]{:S(2)}) collective-permute-start(f32[6,8,256]{2,1,0:T(8,128)S(1)} %get-tuple-element.22), channel_id=1, source_target_pairs={{0,1},{4,5},{8,9},{12,13},{16,17},{20,21},{24,25},{28,29},{1,0},{5... | collective-permute-start | bytes 147464 | tf_op jit(solution)/shard_map/ppermute | solution.py:622
  38.6 0.6 %collective-permute-start.1 = (f32[6,8,256]{2,1,0:T(8,128)S(1)}, f32[6,8,256]{2,1,0:T(8,128)S(1)}, u32[]{:S(2)}, u32[]{:S(2)}) collective-permute-start(f32[6,8,256]{2,1,0:T(8,128)S(1)} %get-tuple-element.23), channel_id=1, source_target_pairs={{0,4},{4,0},{8,12},{12,8},{16,20},{20,16},{24,28},{28,24},{1,2},{5... | collective-permute-start | bytes 147464 | tf_op jit(solution)/shard_map/ppermute | solution.py:622
  39.2 1.3 %down.1 = (f32[30,128,128]{2,1,0:T(8,128)S(1)}, f32[3,128,256]{2,1,0:T(8,128)}) custom-call(f32[3,128,256]{2,1,0:T(8,128)S(1)} %get-tuple-element.20.image_ref, f32[3,128,256]{2,1,0:T(8,128)S(1)} %get-tuple-element.19.truth_ref), custom_call_target="tpu_custom_call" | custom-call | tf_op jit(solution)/shard_map/down/pallas_call | solution.py:709
  40.4 0.0 collective-permute-done.near_in
  40.4 2.2 %collective-permute-done.1.far_in = f32[6,8,256]{2,1,0:T(8,128)S(1)} collective-permute-done((f32[6,8,256]{2,1,0:T(8,128)S(1)}, f32[6,8,256]{2,1,0:T(8,128)S(1)}, u32[]{:S(2)}, u32[]{:S(2)}) %collective-permute-start.1) | collective-permute-done | bytes 49184 | tf_op jit(solution)/shard_map/ppermute | solution.py:622
  42.7 0.7 %turn.1 = (f32[15,256,128]{2,1,0:T(8,128)S(1)}, f32[15,8,128]{2,1,0:T(8,128)S(1)}, f32[15,8,128]{2,1,0:T(8,128)S(1)}) custom-call(f32[3,128,256]{2,1,0:T(8,128)S(1)} %get-tuple-element.20.image_ref, f32[3,128,256]{2,1,0:T(8,128)S(1)} %get-tuple-element.19.truth_ref, f32[6,8,256]{2,1,0:T(8,128)S(1)} %collective-permute-done.near_in, ...), custom_call_target="tpu_custom_call" | custom-call | tf_op jit(solution)/shard_map/turn/pallas_call | solution.py:721
  43.4 0.6 %collective-permute-start.2 = (f32[15,8,128]{2,1,0:T(8,128)S(1)}, f32[15,8,128]{2,1,0:T(8,128)S(1)}, u32[]{:S(2)}, u32[]{:S(2)}) collective-permute-start(f32[15,8,128]{2,1,0:T(8,128)S(1)} %get-tuple-element.26), channel_id=1, source_target_pairs={{0,4},{1,5},{2,6},{3,7},{4,0},{5,1},{6,2},{7,3},{8,12},{9,13},{10,... | collective-permute-start | bytes 184328 | tf_op jit(solution)/shard_map/ppermute | solution.py:622
  44.0 0.0 collective-permute-start.3
  44.0 1.5 %across.1.sum_ref = f32[256,128]{1,0:T(8,128)S(1)} custom-call(f32[15,256,128]{2,1,0:T(8,128)S(1)} %get-tuple-element.25.turned_ref), custom_call_target="tpu_custom_call" | custom-call | tf_op jit(solution)/shard_map/across/pallas_call | solution.py:729
  45.5 2.2 %collective-permute-done.2.near_in = f32[15,8,128]{2,1,0:T(8,128)S(1)} collective-permute-done((f32[15,8,128]{2,1,0:T(8,128)S(1)}, f32[15,8,128]{2,1,0:T(8,128)S(1)}, u32[]{:S(2)}, u32[]{:S(2)}) %collective-permute-start.2) | collective-permute-done | bytes 61472 | tf_op jit(solution)/shard_map/ppermute | solution.py:622
  47.7 0.0 collective-permute-done.3.far_in
  47.7 1.0 %loss.1 = f32[128,256]{1,0:T(8,128)} custom-call(f32[15,256,128]{2,1,0:T(8,128)S(1)} %get-tuple-element.25.turned_ref, f32[15,8,128]{2,1,0:T(8,128)S(1)} %collective-permute-done.2.near_in, f32[15,8,128]{2,1,0:T(8,128)S(1)} %collective-permute-done.3.far_in, f32[256,128]{1,0:T(8,128)S(1)} %across.1.sum_ref, f32[3,128,256]{2,1,0:T(8,128)S(1)} %get-tuple-element.20.image_ref, ...), custom_call_target="tpu_custom_call" | custom-call | tf_op jit(solution)/shard_map/loss/pallas_call | solution.py:730
Async XLA Ops:
  3.3 15.5 %all-to-all-start = ((f32[32,8,128]{2,1,0:T(8,128)}), f32[32,8,128]{2,1,0:T(8,128)S(1)}, u32[]{:S(2)}, u32[]{:S(2)}) async-start(f32[32,8,128]{2,1,0:T(8,128)} %pack.1), calls=%async_computation | async-start | bytes 262144 | tf_op jit(solution)/shard_map/all_to_all | solution.py:658
  10.6 1.0 %copy-start = (f32[3,128,256]{2,1,0:T(8,128)S(1)}, f32[3,128,256]{2,1,0:T(8,128)}, u32[]{:S(2)}) copy-start(f32[3,128,256]{2,1,0:T(8,128)} %truth_in.1) | copy-start | bytes 1179652
  11.6 1.0 %copy-start.1 = (bf16[256,768]{1,0:T(8,128)(2,1)S(1)}, bf16[256,768]{1,0:T(8,128)(2,1)}, u32[]{:S(2)}) copy-start(bf16[256,768]{1,0:T(8,128)(2,1)} %constant.2.clone.basis_in) | copy-start | bytes 1179652
  12.6 0.9 %copy-start.2 = (s32[8,16,512]{2,1,0:T(8,128)S(1)}, s32[8,16,512]{2,1,0:T(8,128)}, u32[]{:S(2)}) copy-start(s32[8,16,512]{2,1,0:T(8,128)} %param.7) | copy-start | bytes 786436
  35.7 4.7 %collective-permute-start = (f32[6,8,256]{2,1,0:T(8,128)S(1)}, f32[6,8,256]{2,1,0:T(8,128)S(1)}, u32[]{:S(2)}, u32[]{:S(2)}) collective-permute-start(f32[6,8,256]{2,1,0:T(8,128)S(1)} %get-tuple-element.22), channel_id=1, source_target_pairs={{0,1},{4,5},{8,9},{12,13},{16,17},{20,21},{24,25},{28,29},{1,0},{5... | collective-permute-start | bytes 147464 | tf_op jit(solution)/shard_map/ppermute | solution.py:622
  38.6 4.1 %collective-permute-start.1 = (f32[6,8,256]{2,1,0:T(8,128)S(1)}, f32[6,8,256]{2,1,0:T(8,128)S(1)}, u32[]{:S(2)}, u32[]{:S(2)}) collective-permute-start(f32[6,8,256]{2,1,0:T(8,128)S(1)} %get-tuple-element.23), channel_id=1, source_target_pairs={{0,4},{4,0},{8,12},{12,8},{16,20},{20,16},{24,28},{28,24},{1,2},{5... | collective-permute-start | bytes 147464 | tf_op jit(solution)/shard_map/ppermute | solution.py:622
  43.4 4.3 %collective-permute-start.2 = (f32[15,8,128]{2,1,0:T(8,128)S(1)}, f32[15,8,128]{2,1,0:T(8,128)S(1)}, u32[]{:S(2)}, u32[]{:S(2)}) collective-permute-start(f32[15,8,128]{2,1,0:T(8,128)S(1)} %get-tuple-element.26), channel_id=1, source_target_pairs={{0,4},{1,5},{2,6},{3,7},{4,0},{5,1},{6,2},{7,3},{8,12},{9,13},{10,... | collective-permute-start | bytes 184328 | tf_op jit(solution)/shard_map/ppermute | solution.py:622
  44.0 3.6 %collective-permute-start.3 = (f32[15,8,128]{2,1,0:T(8,128)S(1)}, f32[15,8,128]{2,1,0:T(8,128)S(1)}, u32[]{:S(2)}, u32[]{:S(2)}) collective-permute-start(f32[15,8,128]{2,1,0:T(8,128)S(1)} %get-tuple-element.27), channel_id=1, source_target_pairs={{0,1},{1,0},{2,3},{3,2},{4,8},{5,9},{6,10},{7,11},{8,4},{9,5},{10,... | collective-permute-start | bytes 184328 | tf_op jit(solution)/shard_map/ppermute | solution.py:622
